TPU v7x, 128 devices: a whole 4x4x4 slice. The times are simulated.
128 devices in a mesh: bucket: 8 (over y, core), member: 16 (over z, x).
Axes of the slice: x: 4, y: 4, z: 4, core: 2. Of those that a mesh axis runs over, the one named last changes fastest.
Arguments:
- loader_rows: float32 [8192, 4096], P(('bucket', 'member')), may hold values from -12 to 12
- dest_bucket: int32 [8192], P(('bucket', 'member')), may hold values from 0 to 7, as said below
- dest_slot: int32 [8192], P(('bucket', 'member')), may hold values from 0 to 127, as said below
- noise: float32 [32768, 4096], P(('bucket', 'member')), may hold values from -12 to 12
Outputs:
- targets: float32 [32768, 4096], P(('bucket', 'member'))
Inputs may be any that keep to these rules, and one draw needn't show every extreme that they name: Loaded row r goes to bucket group dest_bucket[r] on the device of that group with the same member index as its loader device. No loader device sends more than 16 rows to one bucket group; on every member index one bucket group receives exactly 16 rows from every loader device, and every bucket group is so filled on some member index. `dest_slot`: rows that reach the same device have distinct slots.
All inputs are finite; a program needn't handle non-finite values.
Results may differ from a plain program's by a relative error of at most 0.012.
The roundings to bfloat16 on the way count: a program that leaves them out, or rounds other values in their place, can miss the bound.
Values may be sent and summed in bfloat16 or wider, within the bound.
A program may use at most 128 MiB of HBM per device.

v0:
```python
import math
import jax
import jax.numpy as jnp
from jax import lax
from jax.sharding import PartitionSpec as P

ROWS_DEV = 128
ITERS = 4


def tile_cost(panel, noise_rows, noise_norm, width):
    cross_term = lax.dot_general(
        panel, noise_rows, (((1,), (1,)), ((), ())), preferred_element_type=jnp.float32
    )
    panel_wide = panel.astype(jnp.float32)
    return (
        jnp.sum(panel_wide * panel_wide, axis=1)[:, None] + noise_norm[None, :] - 2.0 * cross_term
    ) / width


def body(loader_rows, dest_bucket, dest_slot, noise):
    groups = lax.axis_size("bucket")
    width = loader_rows.shape[1]
    noise_count = noise.shape[0]
    capacity = ROWS_DEV // groups
    epsilon = 0.64 / math.sqrt(width)
    rounded = loader_rows.astype(jnp.bfloat16)
    hits = (dest_bucket[:, None] == jnp.arange(groups, dtype=jnp.int32)[None, :]).astype(jnp.int32)
    ranks = jnp.sum((jnp.cumsum(hits, axis=0) - 1) * hits, axis=1)
    position = dest_bucket * capacity + ranks
    send_rows = jnp.zeros((groups * capacity, width), jnp.bfloat16).at[position].set(rounded)
    send_slots = jnp.full((groups * capacity,), ROWS_DEV, jnp.int32).at[position].set(dest_slot)
    got_rows, got_slots = (
        lax.all_to_all(send_rows, "bucket", split_axis=0, concat_axis=0, tiled=True),
        lax.all_to_all(send_slots, "bucket", split_axis=0, concat_axis=0, tiled=True),
    )
    data_rows = jnp.zeros((ROWS_DEV, width), jnp.bfloat16).at[got_slots].set(got_rows, mode="drop")
    live_rows = (
        jnp.zeros((ROWS_DEV,), jnp.bfloat16)
        .at[got_slots]
        .set(jnp.ones(got_slots.shape, jnp.bfloat16), mode="drop")
    )
    noise_rows = noise.astype(jnp.bfloat16)
    noise_wide = noise_rows.astype(jnp.float32)
    noise_norm = jnp.sum(noise_wide * noise_wide, axis=1)
    whole_rows, whole_live = (
        lax.all_gather(data_rows, "member", axis=0, tiled=True),
        lax.all_gather(live_rows, "member", axis=0, tiled=True),
    )
    cost_tile = tile_cost(whole_rows, noise_rows, noise_norm, width)
    alive_rows = whole_live > 0.5
    col_pot = jnp.zeros((noise_count,), jnp.float32)
    exponent = jnp.zeros(cost_tile.shape, jnp.float32)
    col_total = jnp.ones((noise_count,), jnp.float32)
    for sweep_index in range(ITERS):
        scores = (col_pot[None, :] - cost_tile) / epsilon
        local_peak = jnp.max(scores, axis=1)
        row_peak = lax.pmax(local_peak, "member")
        row_total = lax.psum(jnp.sum(jnp.exp(scores - row_peak[:, None]), axis=1), "member")
        row_pot = -epsilon * (row_peak + jnp.log(row_total))
        col_scores = (row_pot[:, None] - cost_tile) / epsilon
        col_peak = jnp.max(jnp.where(alive_rows[:, None], col_scores, -jnp.inf), axis=0)
        exponent = jnp.where(alive_rows[:, None], jnp.exp(col_scores - col_peak[None, :]), 0.0)
        col_total = jnp.sum(exponent, axis=0)
        col_pot = -epsilon * (col_peak + jnp.log(col_total))
    weights = (exponent / col_total[None, :]).astype(jnp.bfloat16)
    targets = lax.dot_general(
        weights, whole_rows, (((0,), (0,)), ((), ())), preferred_element_type=jnp.float32
    )
    return targets


def solution(mesh):
    return jax.shard_map(
        body,
        mesh=mesh,
        in_specs=(
            P(("bucket", "member"), None),
            P(("bucket", "member")),
            P(("bucket", "member")),
            P(("bucket", "member"), None),
        ),
        out_specs=P(("bucket", "member"), None),
        check_vma=False,
    )
```

profile of v0, /device:TPU:2, one launch (start us, length us, event | category | flops | bytes accessed | tf_op | source)
XLA Modules:
  0.0 500.6 jit_solution(14216818540153028822)
XLA Ops:
  6.5 0.7 fusion.20
  7.3 0.1 reduce_window_sum.11
  7.4 0.8 select_reduce_fusion.7
  8.2 0.7 compare_select_fusion.1
  8.9 0.9 scatter_custom_fusion
  9.8 0.7 all_to_all.16
  10.5 4.5 all-to-all-start
  14.9 3.1 scatter_custom_fusion.2
  18.0 2.2 all-to-all-done
  20.2 3.6 all-to-all-start.1
  23.8 0.0 all-gather.3.cloned.1.call-start
  23.8 0.6 broadcast.141
  24.4 0.7 reduce.3
  25.1 0.1 all_to_all.18
  25.2 14.4 %all-to-all-done.1 = bf16[8,16,4096]{2,1,0:T(8,128)(2,1)S(1)} async-done(((bf16[8,16,4096]{2,1,0:T(8,128)(2,1)}), bf16[8,16,4096]{2,1,0:T(8,128)(2,1)S(1)}, u32[]{:S(2)}, u32[]{:S(2)}) %all-to-all-start.1) | async-done | bytes 1048608 | tf_op jit(solution)/shard_map/all_to_all | solution.py:34
  39.6 3.0 scatter_custom_fusion.3
  42.7 0.0 all-gather.3.cloned.1.call-update
  42.7 2.6 multiply_reduce_fusion.1
  45.3 1.3 scatter_custom_fusion.1
  46.6 21.6 %all-gather = bf16[16,1,128]{2,1,0:T(2,128)(2,1)S(1)} all-gather(bf16[1,1,128]{2,1,0:T(2,128)(2,1)S(1)} %bitcast.16), channel_id=1, replica_groups=mesh['bucket'=8,'member'=16] {'member'}, dimensions={0}, use_global_device_ids=true | all-gather | bytes 4352 | tf_op jit(solution)/shard_map/all_gather | solution.py:48
  68.2 86.4 %all-gather.3.cloned.1.call-done = bf16[2048,4096]{1,0:T(8,128)(2,1)} async-done(((bf16[128,4096]{1,0:T(8,128)(2,1)}), bf16[2048,4096]{1,0:T(8,128)(2,1)}) %all-gather.3.cloned.1.call-update) | async-done | bytes 16777232 | tf_op jit(solution)/shard_map/all_gather | solution.py:47
  154.6 0.0 copy-start
  154.6 7.5 %multiply_reduce_fusion = f32[2048]{0:T(1024)S(1)} fusion(bf16[2048,4096]{1,0:T(8,128)(2,1)} %all-gather.3.cloned.1.call-done), kind=kLoop, calls=%fused_computation.4 | loop fusion | flops 25163776 | bytes 16785408 | tf_op jit(solution)/shard_map/reduce_sum | solution.py:17
  162.1 3.1 copy-done
  165.3 7.8 %fusion.2 = (f32[2048]{0:T(1024)S(1)}, f32[2048,256]{1,0:T(8,128)S(1)}) fusion(bf16[2048,4096]{1,0:T(8,128)(2,1)S(1)} %copy-done, f32[256,4096]{1,0:T(8,128)} %param.7, f32[256]{0:T(256)S(1)} %multiply_reduce_fusion.1, f32[2048]{0:T(1024)S(1)} %multiply_reduce_fusion), kind=kOutput, calls=%fused_computation.30 | convolution fusion | flops 4299683840 | bytes 23086080 | tf_op jit(solution)/shard_map/dot_general | solution.py:12
  173.1 36.8 %pmax.28 = f32[2048]{0:T(1024)S(1)} all-reduce(f32[2048]{0:T(1024)S(1)} %get-tuple-element.5), channel_id=1, replica_groups=mesh['bucket'=8,'member'=16] {'member'}, use_global_device_ids=true, to_apply=%region_9.10 | all-reduce | flops 2048 | bytes 16384 | tf_op jit(solution)/shard_map/pmax | solution.py:58
  209.9 0.8 exponential_reduce_fusion.3
  210.7 38.9 %psum.28 = f32[2048]{0:T(1024)S(1)} all-reduce(f32[2048]{0:T(1024)S(1)} %exponential_reduce_fusion.3), channel_id=1, replica_groups=mesh['bucket'=8,'member'=16] {'member'}, use_global_device_ids=true, to_apply=%region_11.12 | all-reduce | flops 2048 | bytes 16384 | tf_op jit(solution)/shard_map/psum | solution.py:59
  249.6 0.7 select_reduce_fusion.6
  250.3 0.7 select_reduce_fusion.5
  251.0 0.3 fusion.3
  251.4 36.0 %pmax.29 = f32[2048]{0:T(1024)S(1)} all-reduce(f32[2048]{0:T(1024)S(1)} %fusion.3), channel_id=1, replica_groups=mesh['bucket'=8,'member'=16] {'member'}, use_global_device_ids=true, to_apply=%region_15.16 | all-reduce | flops 2048 | bytes 16384 | tf_op jit(solution)/shard_map/pmax | solution.py:58
  287.4 0.8 exponential_reduce_fusion.2
  288.2 38.0 %psum.29 = f32[2048]{0:T(1024)S(1)} all-reduce(f32[2048]{0:T(1024)S(1)} %exponential_reduce_fusion.2), channel_id=1, replica_groups=mesh['bucket'=8,'member'=16] {'member'}, use_global_device_ids=true, to_apply=%region_17.18 | all-reduce | flops 2048 | bytes 16384 | tf_op jit(solution)/shard_map/psum | solution.py:59
  326.2 0.7 select_reduce_fusion.4
  326.9 0.7 select_reduce_fusion.3
  327.6 0.3 fusion.4
  328.0 36.0 %pmax.30 = f32[2048]{0:T(1024)S(1)} all-reduce(f32[2048]{0:T(1024)S(1)} %fusion.4), channel_id=1, replica_groups=mesh['bucket'=8,'member'=16] {'member'}, use_global_device_ids=true, to_apply=%region_21.22 | all-reduce | flops 2048 | bytes 16384 | tf_op jit(solution)/shard_map/pmax | solution.py:58
  364.0 0.8 exponential_reduce_fusion.1
  364.8 38.0 %psum.30 = f32[2048]{0:T(1024)S(1)} all-reduce(f32[2048]{0:T(1024)S(1)} %exponential_reduce_fusion.1), channel_id=1, replica_groups=mesh['bucket'=8,'member'=16] {'member'}, use_global_device_ids=true, to_apply=%region_23.24 | all-reduce | flops 2048 | bytes 16384 | tf_op jit(solution)/shard_map/psum | solution.py:59
  402.9 0.7 select_reduce_fusion.2
  403.6 0.7 select_reduce_fusion.1
  404.3 0.3 fusion.5
  404.7 36.0 %pmax.31 = f32[2048]{0:T(1024)S(1)} all-reduce(f32[2048]{0:T(1024)S(1)} %fusion.5), channel_id=1, replica_groups=mesh['bucket'=8,'member'=16] {'member'}, use_global_device_ids=true, to_apply=%region_27.28 | all-reduce | flops 2048 | bytes 16384 | tf_op jit(solution)/shard_map/pmax | solution.py:58
  440.7 0.8 exponential_reduce_fusion
  441.5 38.2 %psum.31 = f32[2048]{0:T(1024)S(1)} all-reduce(f32[2048]{0:T(1024)S(1)} %exponential_reduce_fusion), channel_id=1, replica_groups=mesh['bucket'=8,'member'=16] {'member'}, use_global_device_ids=true, to_apply=%region_29.30 | all-reduce | flops 2048 | bytes 16384 | tf_op jit(solution)/shard_map/psum | solution.py:59
  479.7 0.7 select_reduce_fusion
  480.5 0.7 fusion.6
  481.2 12.6 %fusion.7 = f32[256,4096]{1,0:T(8,128)} fusion(bf16[2048,4096]{1,0:T(8,128)(2,1)} %all-gather.3.cloned.1.call-done, f32[2048,256]{1,0:T(8,128)S(1)} %get-tuple-element.6, f32[256]{0:T(256)S(1)} %fusion.6, f32[256]{0:T(256)S(1)} %select_reduce_fusion, f32[2048]{0:T(1024)S(1)} %add_multiply_fusion, pred[2048]{0:T(1024)(128)(4,1)S(1)} %compare_bitcast_fusion), kind=kOutput, calls=%fused_computation.35 | convolution fusion | flops 4298113024 | bytes 23080960 | tf_op jit(solution)/shard_map/dot_general | solution.py:67
  (10 shorter events, 0.1 us)
Async XLA Ops:
  10.5 9.7 %all-to-all-start = ((s32[8,16,1]{1,2,0:T(1,128)}), s32[8,16,1]{1,2,0:T(1,128)S(1)}, u32[]{:S(2)}, u32[]{:S(2)}) async-start(s32[8,16,1]{1,2,0:T(1,128)} %bitcast), calls=%async_computation | async-start | bytes 8192 | tf_op jit(solution)/shard_map/all_to_all | solution.py:35
  20.2 19.5 %all-to-all-start.1 = ((bf16[8,16,4096]{2,1,0:T(8,128)(2,1)}), bf16[8,16,4096]{2,1,0:T(8,128)(2,1)S(1)}, u32[]{:S(2)}, u32[]{:S(2)}) async-start(bf16[8,16,4096]{2,1,0:T(8,128)(2,1)} %bitcast.4), calls=%async_computation.1 | async-start | bytes 2097152 | tf_op jit(solution)/shard_map/all_to_all | solution.py:34
  23.8 130.8 %all-gather.3.cloned.1.call-start = ((), (), s32[]{:S(2)}) async-start(), calls=%async_computation.2 | async-start | bytes 17825792 | tf_op jit(solution)/shard_map/all_gather | solution.py:47
  154.6 10.7 %copy-start = (bf16[2048,4096]{1,0:T(8,128)(2,1)S(1)}, bf16[2048,4096]{1,0:T(8,128)(2,1)}, u32[]{:S(2)}) copy-start(bf16[2048,4096]{1,0:T(8,128)(2,1)} %all-gather.3.cloned.1.call-done) | copy-start | bytes 50331652
Sparse Core Ops, SparseCore 0:
  42.8 111.7 all-gather.2
where the time goes:
time: 501 us
  blocking collectives  319 us (64%)
  waiting for transfers between devices  103 us (21%)
  other arithmetic  26.2 us (5%)
  matrix products  20.4 us (4%)
  between operations  13.7 us (3%)
  local copies, waits for them, and re-layouts  9.75 us (2%)
  starting transfers between devices  8.07 us (2%)
    psum x4, blocking collectives, body(): lax.psum(jnp.sum(jnp.exp(scores - row_peak[:, None]), axis=1), 'member')  153 us
    pmax x4, blocking collectives, body(): row_peak = lax.pmax(local_peak, 'member')  145 us
    all_gather x1, waiting for transfers between devices, body(): lax.all_gather(data_rows, 'member', axis=0, tiled=True)  86.4 us
    all_gather x1, blocking collectives, body(): lax.all_gather(live_rows, 'member', axis=0, tiled=True)  21.6 us
    all_to_all x1, waiting for transfers between devices, body(): lax.all_to_all(send_rows, 'bucket', split_axis=0, concat_axis=0, tiled=True)  14.4 us
    dot_general x1, matrix products, body(): lax.dot_general(weights, whole_rows, (((0,), (0,)), ((), ())), preferred_...  12.6 us
  transfers between devices with their start and end apart: 3, of which 3 were waited for; matrix products, arithmetic and copies ran while one was open for 2% of the time, Pallas kernels for 0%

commit v1 on v0

--- a/solution.py
+++ b/solution.py
@@ -56,7 +56,11 @@
         scores = (col_pot[None, :] - cost_tile) / epsilon
         local_peak = jnp.max(scores, axis=1)
         row_peak = lax.pmax(local_peak, "member")
-        row_total = lax.psum(jnp.sum(jnp.exp(scores - row_peak[:, None]), axis=1), "member")
+
+        def wrap_layers_all(local_values):
+            return jnp.sum(lax.all_gather(local_values, "member"), axis=0)
+
+        row_total = wrap_layers_all(jnp.sum(jnp.exp(scores - row_peak[:, None]), axis=1))
         row_pot = -epsilon * (row_peak + jnp.log(row_total))
         col_scores = (row_pot[:, None] - cost_tile) / epsilon
         col_peak = jnp.max(jnp.where(alive_rows[:, None], col_scores, -jnp.inf), axis=0)

time: 501 us -> 442 us (0.88)
  blocking collectives: 319 us -> 260 us
    psum x4 -> x0, blocking collectives: 153 us -> none  [body(): lax.psum(jnp.sum(jnp.exp(scores - row_peak[:, None]), axis=1), 'member')]
    all_gather x0 -> x4, blocking collectives: none -> 93.5 us  [wrap_layers_all(): return jnp.sum(lax.all_gather(local_values, 'member'), axis=0)]
where the time goes in v1:
time: 442 us; the launch traced here: 441 us
  blocking collectives  260 us (59%)
  waiting for transfers between devices  103 us (23%)
  other arithmetic  26.3 us (6%)
  matrix products  20.4 us (5%)
  between operations  13.7 us (3%)
  local copies, waits for them, and re-layouts  9.86 us (2%)
  starting transfers between devices  8.07 us (2%)
    pmax x4, blocking collectives, body(): row_peak = lax.pmax(local_peak, 'member')  145 us
    all_gather x4, blocking collectives, wrap_layers_all(): return jnp.sum(lax.all_gather(local_values, 'member'), axis=0)  93.5 us
    all_gather x1, waiting for transfers between devices, body(): lax.all_gather(data_rows, 'member', axis=0, tiled=True)  86.4 us
    all_gather x1, blocking collectives, body(): lax.all_gather(live_rows, 'member', axis=0, tiled=True)  21.6 us
    all_to_all x1, waiting for transfers between devices, body(): lax.all_to_all(send_rows, 'bucket', split_axis=0, concat_axis=0, tiled=True)  14.4 us
    dot_general x1, matrix products, body(): lax.dot_general(weights, whole_rows, (((0,), (0,)), ((), ())), preferred_...  12.6 us
  transfers between devices with their start and end apart: 3, of which 3 were waited for; matrix products, arithmetic and copies ran while one was open for 2% of the time, Pallas kernels for 0%

profile of v1, /device:TPU:2, one launch (start us, length us, event | category | flops | bytes accessed | tf_op | source)
XLA Modules:
  0.0 441.3 jit_solution(903284111159033024)
XLA Ops:
  6.5 0.7 fusion.20
  7.3 0.1 reduce_window_sum.11
  7.4 0.8 select_reduce_fusion.7
  8.2 0.7 compare_select_fusion.1
  8.9 0.9 scatter_custom_fusion
  9.8 0.7 all_to_all.16
  10.5 4.5 %all-to-all-start = ((s32[8,16,1]{1,2,0:T(1,128)}), s32[8,16,1]{1,2,0:T(1,128)S(1)}, u32[]{:S(2)}, u32[]{:S(2)}) async-start(s32[8,16,1]{1,2,0:T(1,128)} %bitcast), calls=%async_computation | async-start | bytes 8192 | tf_op jit(solution)/shard_map/all_to_all | solution.py:35
  14.9 3.1 scatter_custom_fusion.2
  18.0 2.2 all-to-all-done
  20.2 3.6 all-to-all-start.1
  23.8 0.0 all-gather.7.cloned.1.call-start
  23.8 0.6 broadcast.141
  24.4 0.7 reduce.3
  25.1 0.1 all_to_all.18
  25.2 14.4 %all-to-all-done.1 = bf16[8,16,4096]{2,1,0:T(8,128)(2,1)S(1)} async-done(((bf16[8,16,4096]{2,1,0:T(8,128)(2,1)}), bf16[8,16,4096]{2,1,0:T(8,128)(2,1)S(1)}, u32[]{:S(2)}, u32[]{:S(2)}) %all-to-all-start.1) | async-done | bytes 1048608 | tf_op jit(solution)/shard_map/all_to_all | solution.py:34
  39.6 3.0 scatter_custom_fusion.3
  42.7 0.0 all-gather.7.cloned.1.call-update
  42.7 2.6 multiply_reduce_fusion.1
  45.3 1.3 scatter_custom_fusion.1
  46.6 21.6 %all-gather.4 = bf16[16,1,128]{2,1,0:T(2,128)(2,1)S(1)} all-gather(bf16[1,1,128]{2,1,0:T(2,128)(2,1)S(1)} %bitcast.16), channel_id=1, replica_groups=mesh['bucket'=8,'member'=16] {'member'}, dimensions={0}, use_global_device_ids=true | all-gather | bytes 4352 | tf_op jit(solution)/shard_map/all_gather | solution.py:48
  68.2 86.4 %all-gather.7.cloned.1.call-done = bf16[2048,4096]{1,0:T(8,128)(2,1)} async-done(((bf16[128,4096]{1,0:T(8,128)(2,1)}), bf16[2048,4096]{1,0:T(8,128)(2,1)}) %all-gather.7.cloned.1.call-update) | async-done | bytes 16777232 | tf_op jit(solution)/shard_map/all_gather | solution.py:47
  154.6 0.0 copy-start
  154.6 7.5 %multiply_reduce_fusion = f32[2048]{0:T(1024)S(1)} fusion(bf16[2048,4096]{1,0:T(8,128)(2,1)} %all-gather.7.cloned.1.call-done), kind=kLoop, calls=%fused_computation.4 | loop fusion | flops 25163776 | bytes 16785408 | tf_op jit(solution)/shard_map/reduce_sum | solution.py:17
  162.1 3.1 copy-done
  165.3 7.8 %fusion.2 = (f32[2048]{0:T(1024)S(1)}, f32[2048,256]{1,0:T(8,128)S(1)}) fusion(bf16[2048,4096]{1,0:T(8,128)(2,1)S(1)} %copy-done, f32[256,4096]{1,0:T(8,128)} %param.7, f32[256]{0:T(256)S(1)} %multiply_reduce_fusion.1, f32[2048]{0:T(1024)S(1)} %multiply_reduce_fusion), kind=kOutput, calls=%fused_computation.30 | convolution fusion | flops 4299683840 | bytes 23086080 | tf_op jit(solution)/shard_map/dot_general | solution.py:12
  173.1 36.8 %pmax.28 = f32[2048]{0:T(1024)S(1)} all-reduce(f32[2048]{0:T(1024)S(1)} %get-tuple-element.5), channel_id=1, replica_groups=mesh['bucket'=8,'member'=16] {'member'}, use_global_device_ids=true, to_apply=%region_9.10 | all-reduce | flops 2048 | bytes 16384 | tf_op jit(solution)/shard_map/pmax | solution.py:58
  209.9 0.8 exponential_reduce_fusion.3
  210.7 23.5 %all-gather = f32[32768]{0:T(1024)S(1)} all-gather(f32[2048]{0:T(1024)S(1)} %exponential_reduce_fusion.3), channel_id=2, replica_groups=mesh['bucket'=8,'member'=16] {'member'}, dimensions={0}, use_global_device_ids=true | all-gather | bytes 139264 | tf_op jit(solution)/shard_map/all_gather | solution.py:61
  234.3 0.7 select_reduce_fusion.6
  235.0 0.7 select_reduce_fusion.5
  235.7 0.3 fusion.3
  236.1 36.0 %pmax.29 = f32[2048]{0:T(1024)S(1)} all-reduce(f32[2048]{0:T(1024)S(1)} %fusion.3), channel_id=1, replica_groups=mesh['bucket'=8,'member'=16] {'member'}, use_global_device_ids=true, to_apply=%region_15.16 | all-reduce | flops 2048 | bytes 16384 | tf_op jit(solution)/shard_map/pmax | solution.py:58
  272.1 0.8 exponential_reduce_fusion.2
  272.9 23.3 %all-gather.1 = f32[32768]{0:T(1024)S(1)} all-gather(f32[2048]{0:T(1024)S(1)} %exponential_reduce_fusion.2), channel_id=3, replica_groups=mesh['bucket'=8,'member'=16] {'member'}, dimensions={0}, use_global_device_ids=true | all-gather | bytes 139264 | tf_op jit(solution)/shard_map/all_gather | solution.py:61
  296.3 0.7 select_reduce_fusion.4
  297.0 0.7 select_reduce_fusion.3
  297.7 0.3 fusion.4
  298.1 36.0 %pmax.30 = f32[2048]{0:T(1024)S(1)} all-reduce(f32[2048]{0:T(1024)S(1)} %fusion.4), channel_id=1, replica_groups=mesh['bucket'=8,'member'=16] {'member'}, use_global_device_ids=true, to_apply=%region_21.22 | all-reduce | flops 2048 | bytes 16384 | tf_op jit(solution)/shard_map/pmax | solution.py:58
  334.1 0.8 exponential_reduce_fusion.1
  334.9 23.3 %all-gather.2 = f32[32768]{0:T(1024)S(1)} all-gather(f32[2048]{0:T(1024)S(1)} %exponential_reduce_fusion.1), channel_id=4, replica_groups=mesh['bucket'=8,'member'=16] {'member'}, dimensions={0}, use_global_device_ids=true | all-gather | bytes 139264 | tf_op jit(solution)/shard_map/all_gather | solution.py:61
  358.2 0.7 select_reduce_fusion.2
  358.9 0.7 select_reduce_fusion.1
  359.7 0.3 fusion.5
  360.0 36.0 %pmax.31 = f32[2048]{0:T(1024)S(1)} all-reduce(f32[2048]{0:T(1024)S(1)} %fusion.5), channel_id=1, replica_groups=mesh['bucket'=8,'member'=16] {'member'}, use_global_device_ids=true, to_apply=%region_27.28 | all-reduce | flops 2048 | bytes 16384 | tf_op jit(solution)/shard_map/pmax | solution.py:58
  396.0 0.8 exponential_reduce_fusion
  396.8 23.5 %all-gather.3 = f32[32768]{0:T(1024)S(1)} all-gather(f32[2048]{0:T(1024)S(1)} %exponential_reduce_fusion), channel_id=5, replica_groups=mesh['bucket'=8,'member'=16] {'member'}, dimensions={0}, use_global_device_ids=true | all-gather | bytes 139264 | tf_op jit(solution)/shard_map/all_gather | solution.py:61
  420.4 0.7 select_reduce_fusion
  421.1 0.7 fusion.6
  421.8 12.6 %fusion.7 = f32[256,4096]{1,0:T(8,128)} fusion(bf16[2048,4096]{1,0:T(8,128)(2,1)} %all-gather.7.cloned.1.call-done, f32[2048,256]{1,0:T(8,128)S(1)} %get-tuple-element.6, f32[256]{0:T(256)S(1)} %fusion.6, f32[256]{0:T(256)S(1)} %select_reduce_fusion, f32[2048]{0:T(1024)S(1)} %add_multiply_fusion, pred[2048]{0:T(1024)(128)(4,1)S(1)} %compare_bitcast_fusion), kind=kOutput, calls=%fused_computation.35 | convolution fusion | flops 4298113024 | bytes 23080960 | tf_op jit(solution)/shard_map/dot_general | solution.py:71
  (18 shorter events, 0.3 us)
Async XLA Ops:
  10.5 9.7 %all-to-all-start = ((s32[8,16,1]{1,2,0:T(1,128)}), s32[8,16,1]{1,2,0:T(1,128)S(1)}, u32[]{:S(2)}, u32[]{:S(2)}) async-start(s32[8,16,1]{1,2,0:T(1,128)} %bitcast), calls=%async_computation | async-start | bytes 8192 | tf_op jit(solution)/shard_map/all_to_all | solution.py:35
  20.2 19.5 %all-to-all-start.1 = ((bf16[8,16,4096]{2,1,0:T(8,128)(2,1)}), bf16[8,16,4096]{2,1,0:T(8,128)(2,1)S(1)}, u32[]{:S(2)}, u32[]{:S(2)}) async-start(bf16[8,16,4096]{2,1,0:T(8,128)(2,1)} %bitcast.4), calls=%async_computation.1 | async-start | bytes 2097152 | tf_op jit(solution)/shard_map/all_to_all | solution.py:34
  23.8 130.8 %all-gather.7.cloned.1.call-start = ((), (), s32[]{:S(2)}) async-start(), calls=%async_computation.2 | async-start | bytes 17825792 | tf_op jit(solution)/shard_map/all_gather | solution.py:47
  154.6 10.7 %copy-start = (bf16[2048,4096]{1,0:T(8,128)(2,1)S(1)}, bf16[2048,4096]{1,0:T(8,128)(2,1)}, u32[]{:S(2)}) copy-start(bf16[2048,4096]{1,0:T(8,128)(2,1)} %all-gather.7.cloned.1.call-done) | copy-start | bytes 50331652
Sparse Core Ops, SparseCore 0:
  42.8 111.7 all-gather.6
